TPU v7x, 32 devices: a whole 2x2x4 slice. The times are simulated.
32 devices in a mesh: groups: 2 (over x), dom: 16 (over z, y, core).
Axes of the slice: x: 2, y: 2, z: 4, core: 2. Of those that a mesh axis runs over, the one named last changes fastest.
Arguments:
- particle_places: float32 [16, 3, 3072], P('groups', None, 'dom'), parts along dimension 0, may hold values from 0 to 48, as said below
- particle_speeds: float32 [16, 3, 3072], P('groups', None, 'dom'), parts along dimension 0, may hold values from -7 to 7
- thermal_targets: float32 [16], P('groups'), parts along dimension 0, may hold values from 0.5 to 2
- element_features: bfloat16 [6144, 128], P(('groups', 'dom')), parts along dimension 0, may hold values from -4 to 4
- swap_counterpart_slot: int32 [16], P('groups'), parts along dimension 0, may hold values from 0 to 7, as said below
- swap_approval_flags: int32 [16], P('groups'), parts along dimension 0, may hold values from 0 to 1, as said below
- initial_signal_projector: bfloat16 [128, 128], replicated, may hold values from -0.5 to 0.5
- initial_distance_filter: float32 [8, 128], replicated, may hold values from -2 to 2
- initial_directional_scales: float32 [128], replicated, may hold values from 0.5 to 1.5
- invariant_revision_matrix: bfloat16 [128, 128], replicated, may hold values from -0.5 to 0.5
- magnitude_revision_matrix: bfloat16 [128, 128], replicated, may hold values from -0.5 to 0.5
- later_signal_projector: bfloat16 [128, 128], replicated, may hold values from -0.5 to 0.5
- later_directional_scales: float32 [128], replicated, may hold values from 0.5 to 1.5
- push_output_matrix: float32 [128], replicated, may hold values from -0.5 to 0.5
Outputs:
- positions_new: float32 [16, 3, 3072], P('groups', None, 'dom'), parts along dimension 0
- velocities_new: float32 [16, 3, 3072], P('groups', None, 'dom'), parts along dimension 0
- forces_new: float32 [16, 3, 3072], P('groups', None, 'dom'), parts along dimension 0
There are 2 independent parts, one for each index of `groups`. A program takes and returns all parts, laid end to end along the dimension named above; an argument that names none is the same for every part. Nothing has to cross between parts.
Inputs may be any that keep to these rules, and one draw needn't show every extreme that they name: `particle_places`: the atoms of cell k have x and y in [0, 1) and z in [k, k + 1). `swap_counterpart_slot`: an involution that pairs neighbouring replicas, either (0, 1), (2, 3), ... or (1, 2), (3, 4), ..., a replica left without a pair being its own partner. `swap_approval_flags`: equal for the two replicas of a pair, 0 for a replica that is its own partner.
All inputs are finite; a program needn't handle non-finite values.
Results may differ from a plain program's by a relative error of at most 0.012.
The roundings to bfloat16 on the way count: a program that leaves them out, or rounds other values in their place, can miss the bound.
Values may be sent and summed in bfloat16 or wider, within the bound.
A program may use at most 64 MiB of HBM per device.

v0:
```python
import functools
import math

import jax
import jax.numpy as jnp
from jax import lax
from jax.experimental import pallas as pl
from jax.experimental.pallas import tpu as pltpu
from jax.sharding import PartitionSpec as P

NA = 64
STEPS = 4
LANES = 128
CHUNK = 16
LOG2E = math.log2(math.e)

step_time = 0.05
motion_work_lower_limit = 1e-06

F32 = jnp.float32
BF16 = jnp.bfloat16
MESH = pl.DeviceIdType.MESH
NT = (((1,), (1,)), ((), ()))


def split_bf16(values):
    high = values.astype(BF16)
    low = (values - high.astype(F32)).astype(BF16)
    return high, low


def weight_rows(weights):
    high, low = split_bf16(weights)
    high, low = high.astype(F32), low.astype(F32)
    row = lax.broadcasted_iota(jnp.int32, (16, weights.shape[1]), 0)
    return jnp.where(row == 0, high, jnp.where(row == 1, low, 0.0)).astype(BF16)


def pair_base(rows, columns):
    dx, dy, dz = [row - column for row, column in zip(rows, columns)]
    squared = dx * dx + dy * dy + dz * dz
    inside = jnp.maximum(1.0 - squared, 0.0)
    envelope = inside * inside
    centered = 0.5 - inside
    base = jnp.exp2((centered * centered) * (-98.0 * LOG2E)) * envelope
    return (dx * envelope, dy * envelope, dz * envelope), base, centered


def kernel(
    n, replicas, cells, parts,
    places, speeds, targets, slots, flags, features,
    projector, radial_filter, scales_one, invariant, magnitude, later_projector, scales_two, push,
    places_out, speeds_out, forces_out,
    feature_halo, place_send, place_halo, table_one, table_vec, s_one,
    state_x, state_v, state_g, win, columns, vectors,
    s_send, s_recv, vg_send, vg_recv, kin_send, kin_recv,
    init_send_sem, init_recv_sem, s_send_sem, s_recv_sem, vg_send_sem, vg_recv_sem,
    kin_send_sem, kin_recv_sem,
):
    me = lax.axis_index("dom")
    left = lax.rem(me + n - 1, n)
    right = lax.rem(me + 1, n)
    own = cells * NA
    width = state_x.shape[3]
    group = replicas // parts
    right_at, left_at = own, own + NA
    channels = features.shape[1]

    def cell_at(c):
        return left_at if c < 0 else c * NA

    barrier = pltpu.get_barrier_semaphore()

    def greet(d, carry):
        pl.semaphore_signal(barrier, inc=1, device_id={"dom": lax.rem(me + d, n)}, device_id_type=MESH)
        return carry

    lax.fori_loop(1, n, greet, 0)

    zeros_pad = jnp.zeros((group, width - own), F32)
    for d in range(3):
        x = places[d]
        place_send[d] = jnp.concatenate([x[:, :NA], x[:, own - NA:]], axis=1)
        for p in range(parts):
            members = slice(p * group, (p + 1) * group)
            state_x[p, d] = jnp.concatenate([x[members], zeros_pad], axis=1)
            state_v[p, d] = jnp.concatenate([speeds[d, members, :], zeros_pad], axis=1)
            state_g[p, d] = jnp.zeros((group, width), F32)

    pl.semaphore_wait(barrier, n - 1)

    def remote(src, dst, send_sem, recv_sem, to):
        return pltpu.make_async_remote_copy(
            src_ref=src, dst_ref=dst, send_sem=send_sem, recv_sem=recv_sem,
            device_id={"dom": to}, device_id_type=MESH,
        )

    first = [
        remote(place_send, place_halo.at[1], init_send_sem.at[0], init_recv_sem.at[0], left),
        remote(place_send, place_halo.at[0], init_send_sem.at[1], init_recv_sem.at[1], right),
        remote(features.at[pl.ds(0, NA)], feature_halo.at[1], init_send_sem.at[2], init_recv_sem.at[2], left),
        remote(features.at[pl.ds(own - NA, NA)], feature_halo.at[0], init_send_sem.at[3], init_recv_sem.at[3], right),
    ]
    for copy in first:
        copy.start()

    basis = radial_filter.shape[0]
    offset = lax.broadcasted_iota(jnp.int32, radial_filter.shape, 0).astype(F32) - 0.5 * (basis - 1)
    filters = radial_filter[...] * jnp.exp(-2.0 * offset * offset)
    push_row = push[...]
    w_one = weight_rows(scales_one[...] * push_row)
    w_two = weight_rows(scales_two[...] * push_row)
    scale_row = scales_one[...] * scales_one[...]

    def make_table(rows):
        return jnp.dot(rows, projector[...], preferred_element_type=F32).astype(BF16)

    tables = {c: make_table(features[c * NA:(c + 1) * NA, :]) for c in range(cells)}
    for copy in first:
        copy.wait()
    tables[-1] = make_table(feature_halo[0])
    tables[cells] = make_table(feature_halo[1])

    s_parts = []
    for c in list(range(cells)) + [cells, -1]:
        out = lax.dot_general(w_one, tables[c], NT, preferred_element_type=F32)
        s_parts.append(out[0:1] + out[1:2])
    s_one[...] = jnp.concatenate(s_parts + [jnp.zeros((1, width - own - 2 * NA), F32)], axis=1)

    for c in range(cells):
        before, here, after = [tables[c + j].astype(F32) for j in (-1, 0, 1)]
        table_vec[c, 0:NA, :] = tables[c - 1]
        table_vec[c, NA:2 * NA, :] = tables[c]
        table_vec[c, 2 * NA:3 * NA, :] = tables[c + 1]
        table_vec[c, 3 * NA:4 * NA, :] = jnp.zeros((NA, channels), BF16)
        for k in range(8):
            row = filters[k:k + 1]
            table_one[c, k * LANES:k * LANES + NA, :] = (before * row).astype(BF16)
            table_one[c, k * LANES + NA:(k + 1) * LANES, :] = (here * row).astype(BF16)
        for j in range(4):
            at = (8 + j) * LANES
            table_one[c, at:at + NA, :] = (after * filters[4 + j:5 + j]).astype(BF16)
            table_one[c, at + NA:at + LANES, :] = (after * filters[3 - j:4 - j]).astype(BF16)

    for d in range(3):
        for p in range(parts):
            members = slice(p * group, (p + 1) * group)
            state_x[p, d, :, right_at:right_at + NA] = place_halo[1, d, members, 0:NA]
            state_x[p, d, :, left_at:left_at + NA] = place_halo[0, d, members, NA:2 * NA]

    total = float(cells * n)
    lane = lax.broadcasted_iota(jnp.int32, (1, width), 1)
    up = jnp.where(me == n - 1, total, 0.0).astype(F32)
    down = jnp.where(me == 0, -total, 0.0).astype(F32)
    shift = jnp.where(
        (lane >= right_at) & (lane < right_at + NA), up,
        jnp.where((lane >= left_at) & (lane < left_at + NA), down, 0.0),
    )
    side = jnp.where(lax.broadcasted_iota(jnp.int32, (1, LANES), 1) < NA, 14.0 * LOG2E, -14.0 * LOG2E).astype(F32)
    member_row = lax.broadcasted_iota(jnp.int32, (group, 1), 0)
    replica_row = lax.broadcasted_iota(jnp.int32, (replicas, 1), 0)
    diagonal = (
        lax.broadcasted_iota(jnp.int32, (group, LANES), 0)
        == lax.broadcasted_iota(jnp.int32, (group, LANES), 1)
    )
    target = jnp.zeros((replicas, 1), F32)
    source = jnp.zeros((replicas, 1), jnp.int32)
    for r in range(replicas):
        target = jnp.where(replica_row == r, targets[r], target)
        source = jnp.where(replica_row == r, jnp.where(flags[r] > 0, slots[r], r), source)

    def chain(start, power):
        values = [start]
        for _ in range(3):
            values.append(values[-1] * power)
        return values

    def build(p, c, r):
        rows = [win[p, c, d, r:r + 1, :] for d in range(3)]
        tall = []
        for at in range(0, NA, CHUNK):
            out = slice(at, at + CHUNK)
            cols = [
                columns[p, c * NA + at:c * NA + at + CHUNK, d * group + r:d * group + r + 1]
                for d in range(3)
            ]
            cols = [jnp.broadcast_to(col, (CHUNK, LANES)) for col in cols]
            vec, base, t = pair_base([row[:, :LANES] for row in rows], cols)
            for d in range(3):
                vectors[p, c, r, d * NA + at:d * NA + at + CHUNK, 0:LANES] = vec[d].astype(BF16)
            grow = jnp.exp2((14.0 * LOG2E) * t)
            shrink = jnp.exp2((-14.0 * LOG2E) * t)
            high = chain(base * grow, grow * grow)
            low = chain(base * shrink, shrink * shrink)
            vec, base, t = pair_base([row[:, LANES:] for row in rows], cols)
            for d in range(3):
                vectors[p, c, r, d * NA + at:d * NA + at + CHUNK, LANES:] = vec[d].astype(BF16)
            grow = jnp.exp2(side * t)
            both = chain(base * grow, grow * grow)
            tall.append([x.astype(BF16) for x in low[::-1] + high + both])
        wide = [jnp.concatenate([part[k] for part in tall], axis=0) for k in range(12)]
        return jnp.concatenate(wide, axis=1)

    def layer_one(p, c):
        gauss = jnp.concatenate([build(p, c, r) for r in range(group)], axis=0)
        scalar = jnp.dot(gauss, table_one[c], preferred_element_type=F32).astype(BF16)
        norms = []
        for r in range(group):
            vec = jnp.dot(vectors[p, c, r], table_vec[c], preferred_element_type=F32)
            one, two, three = [vec[d * NA:(d + 1) * NA] for d in range(3)]
            norms.append(((one * one + two * two + three * three) * scale_row).astype(BF16))
        norm = jnp.concatenate(norms, axis=0)
        update = jnp.dot(scalar, invariant[...], preferred_element_type=F32)
        update = update + jnp.dot(norm, magnitude[...], preferred_element_type=F32)
        own_rows = features[c * NA:(c + 1) * NA, :].astype(F32)
        half = 0.5 * update
        hidden = half * jnp.tanh(half) + half + jnp.concatenate([own_rows] * group, axis=0)
        second = jnp.dot(
            hidden.astype(BF16), later_projector[...], preferred_element_type=F32
        ).astype(BF16)
        out = lax.dot_general(w_two, second, NT, preferred_element_type=F32)
        flat = out[0:1] + out[1:2]
        rows = [flat[:, i * NA:(i + 1) * NA] for i in range(group)]
        return jnp.concatenate(rows, axis=0) + s_one[0:1, c * NA:(c + 1) * NA]

    def force(p, c, before, here, after):
        window = jnp.concatenate([before, here, after, jnp.zeros_like(after)], axis=1)
        high, low = split_bf16(window)
        stacked = jnp.concatenate([high.astype(F32), low.astype(F32)] * 2, axis=0).astype(BF16)
        result = jnp.zeros((group, 3 * NA), F32)
        for r in range(group):
            out = lax.dot_general(stacked, vectors[p, c, r], NT, preferred_element_type=F32)
            result = jnp.where(member_row == r, out[:group] + out[group:2 * group], result)
        return result

    order = [0] if cells == 1 else [0, cells - 1] + list(range(1, cells - 1))

    def is_moving(t):
        return jnp.where(t > 0, 1.0, 0.0).astype(F32)

    def s_copies(t, p):
        return [
            remote(s_send.at[t, p], s_recv.at[t, p, 1], s_send_sem.at[t, p, 0], s_recv_sem.at[t, p, 0], left),
            remote(s_send.at[t, p], s_recv.at[t, p, 0], s_send_sem.at[t, p, 1], s_recv_sem.at[t, p, 1], right),
        ]

    def vg_copies(t, p):
        return [
            remote(vg_send.at[t, p, 0], vg_recv.at[t, p, 1], vg_send_sem.at[t, p, 0], vg_recv_sem.at[t, p, 0], left),
            remote(vg_send.at[t, p, 1], vg_recv.at[t, p, 0], vg_send_sem.at[t, p, 1], vg_recv_sem.at[t, p, 1], right),
        ]

    def first_half(t, p):
        moving = is_moving(t)
        places_now = []
        for d in range(3):
            half = state_v[p, d] + (0.5 * step_time) * state_g[p, d]
            x = state_x[p, d] + (moving * step_time) * half
            state_v[p, d] = half
            state_x[p, d] = x
            if d == 2:
                x = x + shift
            places_now.append(x)
        for c in range(cells):
            for d in range(3):
                x = places_now[d]
                pieces = [x[:, at:at + NA] for at in (cell_at(c - 1), cell_at(c), cell_at(c + 1))]
                win[p, c, d, :, :] = jnp.concatenate(pieces + pieces[2:], axis=1)
        tall = jnp.concatenate(places_now + [jnp.zeros((-3 * group % 8, width), F32)], axis=0)
        for at in range(0, own, LANES):
            columns[p, at:at + LANES, :] = tall[:, at:at + LANES].T
        sources = {}
        sent = False
        for c in order:
            sources[c] = layer_one(p, c)
            if not sent and 0 in sources and cells - 1 in sources:
                sent = True
                s_send[t, p] = jnp.concatenate([sources[0], sources[cells - 1]], axis=1)
                for copy in s_copies(t, p):
                    copy.start()
        return sources

    def second_half(t, p, sources):
        moving = is_moving(t)
        forces = {}
        for c in order[2:]:
            forces[c] = force(p, c, sources[c - 1], sources[c], sources[c + 1])
        for copy in s_copies(t, p):
            copy.wait()
        sources[-1] = s_recv[t, p, 0, :, NA:2 * NA]
        sources[cells] = s_recv[t, p, 1, :, 0:NA]
        for c in order[:2]:
            forces[c] = force(p, c, sources[c - 1], sources[c], sources[c + 1])
        kinetic = jnp.zeros((group, 1), F32)
        for d in range(3):
            g = jnp.concatenate([forces[c][:, d * NA:(d + 1) * NA] for c in range(cells)], axis=1)
            v = state_v[p, d, :, 0:own] + (moving * (0.5 * step_time)) * g
            vg_send[t, p, 0, d] = jnp.concatenate([v[:, :NA], g[:, :NA]], axis=1)
            vg_send[t, p, 1, d] = jnp.concatenate([v[:, own - NA:], g[:, own - NA:]], axis=1)
            kinetic = kinetic + jnp.sum(v * v, axis=1, keepdims=True)
            state_v[p, d, :, 0:own] = v
            state_g[p, d, :, 0:own] = g
        across = jnp.sum(jnp.where(diagonal, kinetic, 0.0), axis=0, keepdims=True)
        kin_send[t, p] = across
        kin_recv[t, p, n - 1] = across

        def spread(d, inner):
            remote(
                kin_send.at[t, p], kin_recv.at[t, p, d - 1], kin_send_sem.at[t, p],
                kin_recv_sem.at[t, p], lax.rem(me + d, n),
            ).start()
            return inner

        lax.fori_loop(1, n, spread, 0)
        for copy in vg_copies(t, p):
            copy.start()

    def finish(t, p):
        everything = kin_recv.at[t, p, pl.ds(0, n - 1)]
        for copy in vg_copies(t, p):
            copy.wait()
        pltpu.make_async_copy(everything, everything, kin_send_sem.at[t, p]).wait()
        pltpu.make_async_copy(everything, everything, kin_recv_sem.at[t, p]).wait()
        collected = jnp.sum(kin_recv[t, p], axis=0)
        gathered = jnp.sum(jnp.where(diagonal, collected, 0.0), axis=1, keepdims=True)
        goal = target[p * group:(p + 1) * group]
        stretch = jnp.sqrt(goal / (gathered / (3.0 * own * n) + motion_work_lower_limit))
        stretch = jnp.where(t > 0, stretch, 1.0)
        rest = jnp.zeros((group, width - own - 2 * NA), F32)
        for d in range(3):
            from_left, from_right = vg_recv[t, p, 0, d], vg_recv[t, p, 1, d]
            state_v[p, d] = stretch * jnp.concatenate(
                [state_v[p, d, :, 0:own], from_right[:, :NA], from_left[:, :NA], rest], axis=1
            )
            state_g[p, d, :, right_at:right_at + NA] = from_right[:, NA:]
            state_g[p, d, :, left_at:left_at + NA] = from_left[:, NA:]

    def step(t, carry):
        sources = []
        for p in range(parts):
            pl.when(t > 0)(functools.partial(finish, t - 1, p))
            sources.append(first_half(t, p))
        for p in range(parts):
            second_half(t, p, sources[p])
        return carry

    lax.fori_loop(0, STEPS + 1, step, 0)
    for p in range(parts):
        finish(STEPS, p)

    def pick(values):
        result = jnp.zeros_like(values)
        for r in range(replicas):
            result = jnp.where(source == r, values[r:r + 1], result)
        return result

    def whole(state, d):
        return jnp.concatenate([state[p, d, :, 0:own] for p in range(parts)], axis=0)

    heat = jnp.sqrt(target / pick(target))
    floor = (
        me * cells + lax.broadcasted_iota(jnp.int32, (1, own), 1) // NA
    ).astype(F32)
    for d in range(3):
        x = pick(whole(state_x, d))
        if d == 2:
            x = x - floor
        places_out[d] = x
        speeds_out[d] = pick(whole(state_v, d)) * heat
        forces_out[d] = pick(whole(state_g, d))


def on_device(
    particle_places,
    particle_speeds,
    thermal_targets,
    element_features,
    swap_counterpart_slot,
    swap_approval_flags,
    initial_signal_projector,
    initial_distance_filter,
    initial_directional_scales,
    invariant_revision_matrix,
    magnitude_revision_matrix,
    later_signal_projector,
    later_directional_scales,
    push_output_matrix,
):
    n = lax.axis_size("dom")
    replicas, _, own = particle_places.shape
    cells = own // NA
    channels = element_features.shape[1]
    width = -(-(own + 2 * NA) // LANES) * LANES
    padded = -(-own // LANES) * LANES
    rounds = STEPS + 1
    parts = 2 if replicas % 2 == 0 else 1
    group = replicas // parts
    pad_rows = -(-3 * group // 8) * 8
    basis = initial_distance_filter.shape[0]
    depth = basis * 3 * NA
    vmem = pl.BlockSpec(memory_space=pltpu.VMEM)
    smem = pl.BlockSpec(memory_space=pltpu.SMEM)
    out = jax.ShapeDtypeStruct((3, replicas, own), F32)
    results = pl.pallas_call(
        functools.partial(kernel, n, replicas, cells, parts),
        out_shape=(out, out, out),
        in_specs=[vmem, vmem, smem, smem, smem] + [vmem] * 9,
        out_specs=(vmem, vmem, vmem),
        scratch_shapes=[
            pltpu.VMEM((2, NA, channels), BF16),
            pltpu.VMEM((3, replicas, LANES), F32),
            pltpu.VMEM((2, 3, replicas, LANES), F32),
            pltpu.VMEM((cells, depth, channels), BF16),
            pltpu.VMEM((cells, 4 * NA, channels), BF16),
            pltpu.VMEM((1, width), F32),
            pltpu.VMEM((parts, 3, group, width), F32),
            pltpu.VMEM((parts, 3, group, width), F32),
            pltpu.VMEM((parts, 3, group, width), F32),
            pltpu.VMEM((parts, cells, 3, group, 2 * LANES), F32),
            pltpu.VMEM((parts, padded, pad_rows), F32),
            pltpu.VMEM((parts, cells, group, 3 * NA, 2 * LANES), BF16),
            pltpu.VMEM((rounds, parts, group, LANES), F32),
            pltpu.VMEM((rounds, parts, 2, group, LANES), F32),
            pltpu.VMEM((rounds, parts, 2, 3, group, LANES), F32),
            pltpu.VMEM((rounds, parts, 2, 3, group, LANES), F32),
            pltpu.VMEM((rounds, parts, 1, LANES), F32),
            pltpu.VMEM((rounds, parts, n, 1, LANES), F32),
            pltpu.SemaphoreType.DMA((4,)),
            pltpu.SemaphoreType.DMA((4,)),
            pltpu.SemaphoreType.DMA((rounds, parts, 2)),
            pltpu.SemaphoreType.DMA((rounds, parts, 2)),
            pltpu.SemaphoreType.DMA((rounds, parts, 2)),
            pltpu.SemaphoreType.DMA((rounds, parts, 2)),
            pltpu.SemaphoreType.DMA((rounds, parts)),
            pltpu.SemaphoreType.DMA((rounds, parts)),
        ],
        compiler_params=pltpu.CompilerParams(
            collective_id=0, has_side_effects=True, vmem_limit_bytes=48 * 1024 * 1024
        ),
    )(
        jnp.transpose(particle_places, (1, 0, 2)),
        jnp.transpose(particle_speeds, (1, 0, 2)),
        thermal_targets,
        swap_counterpart_slot,
        swap_approval_flags,
        element_features,
        initial_signal_projector,
        initial_distance_filter,
        initial_directional_scales.reshape(1, -1),
        invariant_revision_matrix,
        magnitude_revision_matrix,
        later_signal_projector,
        later_directional_scales.reshape(1, -1),
        push_output_matrix.reshape(1, -1),
    )
    return tuple(jnp.transpose(result, (1, 0, 2)) for result in results)


def solution(mesh):
    along = P("groups", None, "dom")
    return jax.shard_map(
        on_device,
        mesh=mesh,
        in_specs=(
            along,
            along,
            P("groups"),
            P(("groups", "dom"), None),
            P("groups"),
            P("groups"),
            P(),
            P(),
            P(),
            P(),
            P(),
            P(),
            P(),
            P(),
        ),
        out_specs=(along, along, along),
        check_vma=False,
    )
```

profile of v0, /device:TPU:0, one launch (start us, length us, event | category | flops | bytes accessed | tf_op | source)
XLA Modules:
  0.0 79.7 jit_solution(4369690804673446628)
XLA Ops:
  0.6 0.0 copy-start.7
  0.6 0.0 copy-start.11
  0.7 0.0 copy-start.12
  0.7 0.0 copy-start.13
  0.7 0.0 copy-start.8
  0.7 0.0 copy-start.9
  0.7 0.0 copy-start.10
  0.7 0.6 copy-done.7
  1.3 0.0 copy-done.11
  1.3 0.0 copy-done.12
  1.3 0.0 copy-done.13
  1.3 0.0 copy-done.8
  1.4 0.0 copy-done.9
  1.4 0.0 copy-done.10
  1.4 0.0 copy-start
  1.4 0.8 copy-done
  2.2 0.0 copy-start.1
  2.2 0.8 copy-done.1
  2.9 0.0 copy-start.2
  2.9 0.8 copy-done.2
  3.7 0.0 copy-start.3
  3.7 0.8 copy-done.3
  4.5 0.0 copy-start.4
  4.5 0.8 copy-done.4
  5.2 0.0 copy-start.5
  5.2 0.7 copy-done.5
  6.0 0.0 copy-start.6
  6.0 0.7 copy-done.6
  6.7 71.1 %shard_map.157 = (f32[3,8,192]{2,1,0:T(8,128)S(1)}, f32[3,8,192]{2,1,0:T(8,128)S(1)}, f32[3,8,192]{2,1,0:T(8,128)S(1)}) custom-call(f32[3,8,192]{2,1,0:T(8,128)S(1)} %bitcast.11, f32[3,8,192]{2,1,0:T(8,128)S(1)} %bitcast.12, f32[8]{0:T(128)S(1)} %copy-done.8, s32[8]{0:T(128)S(1)} %copy-done.9, s32[8]{0:T(128)S(1)} %copy-done.10, ...), custom_call_target="tpu_custom_call" | custom-call | tf_op jit(solution)/shard_map/pallas_call | solution.py:404
  77.8 0.6 copy.20
  78.4 0.6 copy.21
  79.1 0.6 copy.22
Async XLA Ops:
  0.6 0.7 copy-start.7
  0.6 0.7 copy-start.11
  0.7 0.7 copy-start.12
  0.7 0.7 copy-start.13
  0.7 0.7 copy-start.8
  0.7 0.7 copy-start.9
  0.7 0.7 copy-start.10
  1.4 0.8 %copy-start = (bf16[192,128]{1,0:T(8,128)(2,1)S(1)}, bf16[192,128]{1,0:T(8,128)(2,1)}, u32[]{:S(2)}) copy-start(bf16[192,128]{1,0:T(8,128)(2,1)} %features.1) | copy-start | bytes 147460
  2.2 0.8 copy-start.1
  2.9 0.8 copy-start.2
  3.7 0.8 copy-start.3
  4.5 0.8 copy-start.4
  5.2 0.7 copy-start.5
  6.0 0.7 copy-start.6
where the time goes:
time: 80.3 us; the launch traced here: 79.7 us
  Pallas kernels  71.1 us (89%)
  local copies, waits for them, and re-layouts  7.82 us (10%)
    pallas_call x1, Pallas kernels, on_device(): pl.pallas_call(functools.partial(kernel, n, replicas, cells, parts), out_...  71.1 us
    unnamed x31, local copies, waits for them, and re-layouts  7.82 us

commit v1 on v0

v1 whole, which is shorter than its diff:
```python
import functools
import math

import jax
import jax.numpy as jnp
from jax import lax
from jax.experimental import pallas as pl
from jax.experimental.pallas import tpu as pltpu
from jax.sharding import PartitionSpec as P

NA = 64
STEPS = 4
LANES = 128
CHUNK = 16
HALO = 2
SPLITS = 3
LOG2E = math.log2(math.e)

step_time = 0.05
motion_work_lower_limit = 1e-06

F32 = jnp.float32
BF16 = jnp.bfloat16
MESH = pl.DeviceIdType.MESH


def split_bf16(values):
    high = values.astype(BF16)
    low = (values - high.astype(F32)).astype(BF16)
    return high, low


def weight_rows(weights):
    high, low = split_bf16(weights)
    high, low = high.astype(F32), low.astype(F32)
    row = lax.broadcasted_iota(jnp.int32, (16, weights.shape[1]), 0)
    return jnp.where(row == 0, high, jnp.where(row == 1, low, 0.0)).astype(BF16)


def swap_halves(values):
    return pltpu.roll(values, NA, 1)


def kernel(
    n, replicas, cells, parts,
    places, speeds, targets, slots, flags, features,
    projector, radial_filter, scales_one, invariant, magnitude, later_projector, scales_two, push,
    places_out, speeds_out, forces_out,
    own_places, own_speeds, feats, w_project, w_filter, w_scale_one, w_invariant, w_magnitude,
    w_later, w_scale_two, w_push,
    place_halo, table_one, table_vec, feat_t, mix, later_t, scale_sq, read_two, s_one, selector,
    state_x, state_v, state_g, cols, xb, gauss, vecs, mixed,
    vg_send, vg_recv, kin_send, kin_recv,
    load_sem, init_send_sem, init_recv_sem, vg_send_sem, vg_recv_sem, kin_send_sem, kin_recv_sem,
):
    me = lax.axis_index("dom")
    left = lax.rem(me + n - 1, n)
    right = lax.rem(me + 1, n)
    own = cells * NA
    edge = HALO * NA
    ext = cells + 2 * HALO
    inner = cells + 2
    wide = state_x.shape[3]
    group = replicas // parts
    lanes = group * NA
    tiles = lanes // LANES
    channels = features.shape[1]
    basis = radial_filter.shape[0]
    near = 3 * NA

    barrier = pltpu.get_barrier_semaphore()

    def greet(d, carry):
        pl.semaphore_signal(barrier, inc=1, device_id={"dom": lax.rem(me + d, n)}, device_id_type=MESH)
        return carry

    loads = [
        (features, feats.at[pl.ds(edge, own)]),
        (projector, w_project),
        (places, own_places),
        (speeds, own_speeds),
        (radial_filter, w_filter),
        (scales_one, w_scale_one),
        (invariant, w_invariant),
        (magnitude, w_magnitude),
        (later_projector, w_later),
        (scales_two, w_scale_two),
        (push, w_push),
    ]
    loads = [pltpu.make_async_copy(src, dst, load_sem.at[i]) for i, (src, dst) in enumerate(loads)]
    for load in loads:
        load.start()
    lax.fori_loop(1, n, greet, 0)

    def remote(src, dst, send_sem, recv_sem, to):
        return pltpu.make_async_remote_copy(
            src_ref=src, dst_ref=dst, send_sem=send_sem, recv_sem=recv_sem,
            device_id={"dom": to}, device_id_type=MESH,
        )

    first = [
        remote(places, place_halo.at[1], init_send_sem.at[0], init_recv_sem.at[0], left),
        remote(places, place_halo.at[0], init_send_sem.at[1], init_recv_sem.at[1], right),
        remote(
            features.at[pl.ds(0, edge)], feats.at[pl.ds(edge + own, edge)],
            init_send_sem.at[2], init_recv_sem.at[2], left,
        ),
        remote(
            features.at[pl.ds(own - edge, edge)], feats.at[pl.ds(0, edge)],
            init_send_sem.at[3], init_recv_sem.at[3], right,
        ),
    ]
    pl.semaphore_wait(barrier, n - 1)
    for copy in first:
        copy.start()
    for load in loads:
        load.wait()

    half_lane = lax.broadcasted_iota(jnp.int32, (1, LANES), 1) < NA
    member_row = lax.broadcasted_iota(jnp.int32, (group, 1), 0)

    def flip(values):
        return values.astype(F32).T

    def column(row):
        return jnp.broadcast_to(row.T[:, 0:1], (channels, LANES))

    offset = lax.broadcasted_iota(jnp.int32, (basis, channels), 0).astype(F32) - 0.5 * (basis - 1)
    filters = (w_filter[...] * jnp.exp(-2.0 * offset * offset)).T
    push_row = w_push[...]
    w_one = weight_rows(w_scale_one[...] * push_row)
    read_two[...] = weight_rows(w_scale_two[...] * push_row)
    scale_row = jnp.broadcast_to(w_scale_one[...] * w_scale_one[...], (8, channels))
    scale_sq[...] = column(scale_row)
    mix[:, 0:channels] = (0.5 * flip(w_invariant[...])).astype(BF16)
    mix[:, channels:2 * channels] = (0.5 * flip(w_magnitude[...])).astype(BF16)
    later_t[...] = flip(w_later[...]).astype(BF16)

    k_row = lax.broadcasted_iota(jnp.int32, (LANES, lanes), 0)
    k_lane = lax.broadcasted_iota(jnp.int32, (LANES, lanes), 1)
    for d in range(3):
        base = d * SPLITS * group
        inside = (k_row >= base) & (k_row < base + SPLITS * group)
        chosen = inside & ((k_row - base) % group == k_lane // NA)
        selector[d] = jnp.where(chosen, 1.0, 0.0).astype(BF16)
    for p in range(parts):
        for i in range(inner):
            for d in range(3):
                vecs[p, i, d, near:, :] = jnp.zeros((4 * NA - near, lanes), BF16)
    feats[ext * NA:, :] = jnp.zeros((wide - ext * NA, channels), BF16)

    total = cells * n
    floor_own = (me * cells).astype(F32)
    floor_left = (me * cells + jnp.where(me == 0, total, 0)).astype(F32)
    floor_right = (me * cells - jnp.where(me == n - 1, total, 0)).astype(F32)
    lift = [0.0, 0.0, 1.0]
    tail = jnp.zeros((group, wide - ext * NA), F32)
    for p in range(parts):
        members = slice(p * group, (p + 1) * group)
        for d in range(3):
            state_v[p, d] = jnp.concatenate(
                [jnp.zeros((group, edge), F32), own_speeds[d, members, :], jnp.zeros((group, edge), F32), tail],
                axis=1,
            )
            state_g[p, d] = jnp.zeros((group, wide), F32)

    for copy in first:
        copy.wait()

    for p in range(parts):
        members = slice(p * group, (p + 1) * group)
        for d in range(3):
            state_x[p, d] = jnp.concatenate(
                [
                    place_halo[0, d, members, own - edge:] - lift[d] * floor_left,
                    own_places[d, members, :] - lift[d] * floor_own,
                    place_halo[1, d, members, :edge] - lift[d] * floor_right,
                    tail,
                ],
                axis=1,
            )

    signals = jnp.dot(feats[...], w_project[...], preferred_element_type=F32).astype(BF16)
    signal_tiles = [flip(signals[at:at + LANES]) for at in range(0, wide, LANES)]
    feat_tiles = [flip(feats[at:at + LANES, :]) for at in range(0, wide, LANES)]

    def double(tile_list, e):
        tile = tile_list[e // 2]
        other = swap_halves(tile)
        return jnp.where(half_lane, tile, other) if e % 2 == 0 else jnp.where(half_lane, other, tile)

    doubles = [double(signal_tiles, e) for e in range(ext)]
    flat_signals = jnp.concatenate(signal_tiles, axis=1).astype(BF16)
    out = jnp.dot(w_one, flat_signals, preferred_element_type=F32)
    s_one[...] = out[0:1] + out[1:2]
    for i in range(inner):
        feat_t[i] = double(feat_tiles, i + 1)
        pair = jnp.where(half_lane, doubles[i], doubles[i + 1])
        table_vec[i, :, 0:LANES] = pair.astype(BF16)
        table_vec[i, :, LANES:2 * LANES] = jnp.where(half_lane, doubles[i + 2], 0.0).astype(BF16)
        for k in range(basis):
            col = jnp.broadcast_to(filters[:, k:k + 1], (channels, LANES))
            table_one[i, :, k * LANES:(k + 1) * LANES] = (pair * col).astype(BF16)
            if k % 2 == 1:
                both = jnp.where(half_lane, jnp.broadcast_to(filters[:, k - 1:k], (channels, LANES)), col)
                at = basis * LANES + (k // 2) * LANES
                table_one[i, :, at:at + LANES] = (doubles[i + 2] * both).astype(BF16)

    replica_row = lax.broadcasted_iota(jnp.int32, (replicas, 1), 0)
    diagonal = (
        lax.broadcasted_iota(jnp.int32, (group, LANES), 0)
        == lax.broadcasted_iota(jnp.int32, (group, LANES), 1)
    )
    target = jnp.zeros((replicas, 1), F32)
    source = jnp.zeros((replicas, 1), jnp.int32)
    for r in range(replicas):
        target = jnp.where(replica_row == r, targets[r], target)
        source = jnp.where(replica_row == r, jnp.where(flags[r] > 0, slots[r], r), source)

    def spread_row(tile_list, e):
        tile = tile_list[e // 2]
        other = swap_halves(tile)
        first_half, second_half = (tile, other) if e % 2 == 0 else (other, tile)
        return [
            jnp.where(half_lane, first_half[2 * m:2 * m + 1], second_half[2 * m + 1:2 * m + 2])
            for m in range(tiles)
        ]

    def gather_rows(values, odd):
        result = None
        for r in range(group):
            tile = values[:, (r // 2) * LANES:(r // 2 + 1) * LANES]
            if (r % 2 == 1) != odd:
                tile = swap_halves(tile)
            result = tile if result is None else jnp.where(member_row == r, tile, result)
        return jnp.broadcast_to(result, (group, LANES))

    def pairs(p, i, place_tiles):
        e = i + 1
        mine = [
            jnp.broadcast_to(jnp.concatenate(spread_row(place_tiles[d], e), axis=1), (CHUNK, lanes))
            for d in range(3)
        ]
        for at in range(0, near, CHUNK):
            row = i * NA + at
            dx, dy, dz = [xb[p, d, row:row + CHUNK, :] - mine[d] for d in range(3)]
            squared = dx * dx + dy * dy + dz * dz
            inside = jnp.maximum(1.0 - squared, 0.0)
            envelope = inside * inside
            for d, step in enumerate((dx, dy, dz)):
                vecs[p, i, d, at:at + CHUNK, :] = (step * envelope).astype(BF16)
            centered = 0.5 - inside
            value = jnp.exp2((centered * (centered + 1.0)) * (-98.0 * LOG2E)) * envelope
            ratio = jnp.exp2(centered * (28.0 * LOG2E))
            for k in range(basis):
                if at < 2 * NA:
                    to = k * LANES + at
                else:
                    to = basis * LANES + k * NA + at - 2 * NA
                gauss[p, i, to:to + CHUNK, :] = value.astype(BF16)
                if k + 1 < basis:
                    value = value * ratio

    def dense(p, i):
        scalar = jnp.dot(table_one[i], gauss[p, i], preferred_element_type=F32)
        mixed[p, i, 0:channels, :] = scalar.astype(BF16)
        norm = None
        for d in range(3):
            vec = jnp.dot(table_vec[i], vecs[p, i, d], preferred_element_type=F32)
            norm = vec * vec if norm is None else norm + vec * vec
        norm = norm * jnp.concatenate([scale_sq[...]] * tiles, axis=1)
        mixed[p, i, channels:, :] = norm.astype(BF16)
        half = jnp.dot(mix[...], mixed[p, i], preferred_element_type=F32)
        hidden = half * jnp.tanh(half) + half + jnp.concatenate([feat_t[i]] * tiles, axis=1)
        second = jnp.dot(later_t[...], hidden.astype(BF16), preferred_element_type=F32).astype(BF16)
        out = jnp.dot(read_two[...], second, preferred_element_type=F32)
        return out[0:1] + out[1:2]

    def force(p, e, strengths):
        window = strengths[:, (e - 1) * NA:(e + 3) * NA]
        high, low = split_bf16(window)
        stacked = jnp.concatenate([high.astype(F32), low.astype(F32)], axis=0)
        stacked = jnp.concatenate([stacked] * (16 // (2 * group)), axis=0).astype(BF16)
        result = []
        for d in range(3):
            out = jnp.dot(stacked, vecs[p, e - 1, d], preferred_element_type=F32)
            result.append(gather_rows(out[:group] + out[group:2 * group], e % 2 == 1))
        return result

    def is_moving(t):
        return jnp.where(t > 0, 1.0, 0.0).astype(F32)

    def vg_copies(t, p):
        return [
            remote(vg_send.at[t, p, 0], vg_recv.at[t, p, 1], vg_send_sem.at[t, p, 0], vg_recv_sem.at[t, p, 0], left),
            remote(vg_send.at[t, p, 1], vg_recv.at[t, p, 0], vg_send_sem.at[t, p, 1], vg_recv_sem.at[t, p, 1], right),
        ]

    def advance(t, p):
        moving = is_moving(t)
        place_tiles = []
        stack = []
        for d in range(3):
            half = state_v[p, d] + (0.5 * step_time) * state_g[p, d]
            x = state_x[p, d] + (moving * step_time) * half
            state_v[p, d] = half
            state_x[p, d] = x
            place_tiles.append([x[:, at:at + LANES] for at in range(0, wide, LANES)])
            rest = x
            for s in range(SPLITS):
                piece = rest.astype(BF16).astype(F32)
                rest = rest - piece
                stack.append(piece)
        stack.append(jnp.zeros((LANES - 3 * SPLITS * group, wide), F32))
        tall = jnp.concatenate(stack, axis=0)
        for at in range(0, wide, LANES):
            cols[p, at:at + LANES, :] = tall[:, at:at + LANES].T.astype(BF16)
        for d in range(3):
            xb[p, d] = jnp.dot(cols[p, 0:ext * NA, :], selector[d], preferred_element_type=F32)
        flats = []
        for i in range(inner):
            pairs(p, i, place_tiles)
            flats.append(dense(p, i))
        strengths = []
        for at in range(0, wide // NA, 2):
            even, odd = [
                gather_rows(flats[e - 1], e % 2 == 1) if 1 <= e <= inner else jnp.zeros((group, LANES), F32)
                for e in (at, at + 1)
            ]
            strengths.append(jnp.where(half_lane, even, odd))
        strengths = jnp.concatenate(strengths, axis=1) + s_one[...]
        pushes = [force(p, e, strengths) for e in range(HALO, HALO + cells)]
        kinetic = jnp.zeros((group, 1), F32)
        for d in range(3):
            joined = []
            for c in range(0, cells, 2):
                even = pushes[c][d]
                odd = pushes[c + 1][d] if c + 1 < cells else jnp.zeros((group, LANES), F32)
                joined.append(jnp.where(half_lane, even, odd))
            g = jnp.concatenate(joined, axis=1)[:, :own]
            v = state_v[p, d, :, edge:edge + own] + (moving * (0.5 * step_time)) * g
            vg_send[t, p, 0, d] = jnp.concatenate([v[:, :edge], g[:, :edge]], axis=1)
            vg_send[t, p, 1, d] = jnp.concatenate([v[:, own - edge:], g[:, own - edge:]], axis=1)
            kinetic = kinetic + jnp.sum(v * v, axis=1, keepdims=True)
            state_v[p, d, :, edge:edge + own] = v
            state_g[p, d, :, edge:edge + own] = g
        across = jnp.sum(jnp.where(diagonal, kinetic, 0.0), axis=0, keepdims=True)
        kin_send[t, p] = across
        kin_recv[t, p, n - 1] = across

        def spread(d, inner_carry):
            remote(
                kin_send.at[t, p], kin_recv.at[t, p, d - 1], kin_send_sem.at[t, p],
                kin_recv_sem.at[t, p], lax.rem(me + d, n),
            ).start()
            return inner_carry

        for copy in vg_copies(t, p):
            copy.start()
        lax.fori_loop(1, n, spread, 0)

    def finish(t, p):
        everything = kin_recv.at[t, p, pl.ds(0, n - 1)]
        for copy in vg_copies(t, p):
            copy.wait()
        pltpu.make_async_copy(everything, everything, kin_send_sem.at[t, p]).wait()
        pltpu.make_async_copy(everything, everything, kin_recv_sem.at[t, p]).wait()
        collected = jnp.sum(kin_recv[t, p], axis=0)
        gathered = jnp.sum(jnp.where(diagonal, collected, 0.0), axis=1, keepdims=True)
        goal = target[p * group:(p + 1) * group]
        stretch = jnp.sqrt(goal / (gathered / (3.0 * own * n) + motion_work_lower_limit))
        stretch = jnp.where(t > 0, stretch, 1.0)
        rest = jnp.zeros((group, wide - ext * NA), F32)
        for d in range(3):
            from_left, from_right = vg_recv[t, p, 0, d], vg_recv[t, p, 1, d]
            state_v[p, d] = stretch * jnp.concatenate(
                [from_left[:, :edge], state_v[p, d, :, edge:edge + own], from_right[:, :edge], rest], axis=1
            )
            state_g[p, d, :, 0:edge] = from_left[:, edge:]
            state_g[p, d, :, edge + own:2 * edge + own] = from_right[:, edge:]

    def step(t, carry):
        for p in range(parts):
            pl.when(t > 0)(functools.partial(finish, t - 1, p))
            advance(t, p)
        return carry

    lax.fori_loop(0, STEPS + 1, step, 0)
    for p in range(parts):
        finish(STEPS, p)

    def pick(values):
        result = jnp.zeros_like(values)
        for r in range(replicas):
            result = jnp.where(source == r, values[r:r + 1], result)
        return result

    def whole(state, d):
        return jnp.concatenate([state[p, d, :, edge:edge + own] for p in range(parts)], axis=0)

    heat = jnp.sqrt(target / pick(target))
    floor = (lax.broadcasted_iota(jnp.int32, (1, own), 1) // NA).astype(F32)
    for d in range(3):
        x = pick(whole(state_x, d))
        if d == 2:
            x = x - floor
        places_out[d] = x
        speeds_out[d] = pick(whole(state_v, d)) * heat
        forces_out[d] = pick(whole(state_g, d))


def on_device(
    particle_places,
    particle_speeds,
    thermal_targets,
    element_features,
    swap_counterpart_slot,
    swap_approval_flags,
    initial_signal_projector,
    initial_distance_filter,
    initial_directional_scales,
    invariant_revision_matrix,
    magnitude_revision_matrix,
    later_signal_projector,
    later_directional_scales,
    push_output_matrix,
):
    n = lax.axis_size("dom")
    replicas, _, own = particle_places.shape
    cells = own // NA
    channels = element_features.shape[1]
    ext = cells + 2 * HALO
    inner = cells + 2
    edge = HALO * NA
    wide = -(-ext * NA // LANES) * LANES
    rounds = STEPS + 1
    group = 4
    parts = replicas // group
    lanes = group * NA
    basis = initial_distance_filter.shape[0]
    depth = basis * 3 * NA
    vmem = pl.BlockSpec(memory_space=pltpu.VMEM)
    smem = pl.BlockSpec(memory_space=pltpu.SMEM)
    outside = pl.BlockSpec(memory_space=pl.ANY)
    out = jax.ShapeDtypeStruct((3, replicas, own), F32)
    results = pl.pallas_call(
        functools.partial(kernel, n, replicas, cells, parts),
        out_shape=(out, out, out),
        in_specs=[outside, outside, smem, smem, smem] + [outside] * 9,
        out_specs=(vmem, vmem, vmem),
        scratch_shapes=[
            pltpu.VMEM((3, replicas, own), F32),
            pltpu.VMEM((3, replicas, own), F32),
            pltpu.VMEM((wide, channels), BF16),
            pltpu.VMEM((channels, channels), BF16),
            pltpu.VMEM((basis, channels), F32),
            pltpu.VMEM((1, channels), F32),
            pltpu.VMEM((channels, channels), BF16),
            pltpu.VMEM((channels, channels), BF16),
            pltpu.VMEM((channels, channels), BF16),
            pltpu.VMEM((1, channels), F32),
            pltpu.VMEM((1, channels), F32),
            pltpu.VMEM((2, 3, replicas, own), F32),
            pltpu.VMEM((inner, channels, depth), BF16),
            pltpu.VMEM((inner, channels, 4 * NA), BF16),
            pltpu.VMEM((inner, channels, LANES), F32),
            pltpu.VMEM((channels, 2 * channels), BF16),
            pltpu.VMEM((channels, channels), BF16),
            pltpu.VMEM((channels, LANES), F32),
            pltpu.VMEM((16, channels), BF16),
            pltpu.VMEM((1, wide), F32),
            pltpu.VMEM((3, LANES, lanes), BF16),
            pltpu.VMEM((parts, 3, group, wide), F32),
            pltpu.VMEM((parts, 3, group, wide), F32),
            pltpu.VMEM((parts, 3, group, wide), F32),
            pltpu.VMEM((parts, wide, LANES), BF16),
            pltpu.VMEM((parts, 3, ext * NA, lanes), F32),
            pltpu.VMEM((parts, inner, depth, lanes), BF16),
            pltpu.VMEM((parts, inner, 3, 4 * NA, lanes), BF16),
            pltpu.VMEM((parts, inner, 2 * channels, lanes), BF16),
            pltpu.VMEM((rounds, parts, 2, 3, group, 2 * edge), F32),
            pltpu.VMEM((rounds, parts, 2, 3, group, 2 * edge), F32),
            pltpu.VMEM((rounds, parts, 1, LANES), F32),
            pltpu.VMEM((rounds, parts, n, 1, LANES), F32),
            pltpu.SemaphoreType.DMA((11,)),
            pltpu.SemaphoreType.DMA((4,)),
            pltpu.SemaphoreType.DMA((4,)),
            pltpu.SemaphoreType.DMA((rounds, parts, 2)),
            pltpu.SemaphoreType.DMA((rounds, parts, 2)),
            pltpu.SemaphoreType.DMA((rounds, parts)),
            pltpu.SemaphoreType.DMA((rounds, parts)),
        ],
        compiler_params=pltpu.CompilerParams(
            collective_id=0, has_side_effects=True, vmem_limit_bytes=63 * 1024 * 1024
        ),
    )(
        jnp.transpose(particle_places, (1, 0, 2)),
        jnp.transpose(particle_speeds, (1, 0, 2)),
        thermal_targets,
        swap_counterpart_slot,
        swap_approval_flags,
        element_features,
        initial_signal_projector,
        initial_distance_filter,
        initial_directional_scales.reshape(1, -1),
        invariant_revision_matrix,
        magnitude_revision_matrix,
        later_signal_projector,
        later_directional_scales.reshape(1, -1),
        push_output_matrix.reshape(1, -1),
    )
    return tuple(jnp.transpose(result, (1, 0, 2)) for result in results)
def solution(mesh):
    along = P("groups", None, "dom")
    return jax.shard_map(
        on_device,
        mesh=mesh,
        in_specs=(
            along,
            along,
            P("groups"),
            P(("groups", "dom"), None),
            P("groups"),
            P("groups"),
            P(),
            P(),
            P(),
            P(),
            P(),
            P(),
            P(),
            P(),
        ),
        out_specs=(along, along, along),
        check_vma=False,
    )
```

time: 80.3 us -> 67.7 us (0.84)
  Pallas kernels: 71.1 us -> 64 us
  local copies, waits for them, and re-layouts: 7.82 us -> 2.71 us
    pallas_call x1, Pallas kernels: 71.1 us -> 64 us  [on_device(): pl.pallas_call(functools.partial(kernel, n, replicas, cells, parts), out_...]
    unnamed x31 -> x7, local copies, waits for them, and re-layouts: 7.82 us -> 2.71 us
where the time goes in v1:
time: 67.7 us; the launch traced here: 67.4 us
  Pallas kernels  64 us (95%)
  local copies, waits for them, and re-layouts  2.71 us (4%)
    pallas_call x1, Pallas kernels, on_device(): pl.pallas_call(functools.partial(kernel, n, replicas, cells, parts), out_...  64 us
    unnamed x7, local copies, waits for them, and re-layouts  2.71 us

profile of v1, /device:TPU:0, one launch (start us, length us, event | category | flops | bytes accessed | tf_op | source)
XLA Modules:
  0.0 67.4 jit_solution(5178878586774309539)
XLA Ops:
  0.6 64.0 %shard_map.157 = (f32[3,8,192]{2,1,0:T(8,128)}, f32[3,8,192]{2,1,0:T(8,128)}, f32[3,8,192]{2,1,0:T(8,128)}) custom-call(f32[3,8,192]{2,1,0:T(8,128)} %bitcast.11, f32[3,8,192]{2,1,0:T(8,128)} %bitcast.12, f32[8]{0:T(128)} %targets.1, s32[8]{0:T(128)} %slots.1, s32[8]{0:T(128)} %flags.1, bf16[192,128]{1,0:T(8,128)(2,1)} %features.1, ...), custom_call_target="tpu_custom_call" | custom-call | tf_op jit(solution)/shard_map/pallas_call | solution.py:446
  64.7 0.0 copy-start.1
  64.7 1.4 %copy.20 = f32[8,3,192]{2,0,1:T(8,128)} copy(f32[8,3,192]{2,0,1:T(8,128)} %bitcast.10) | data formatting | bytes 36864
  66.0 0.0 copy-done.1
  66.0 0.0 copy-start
  66.0 0.6 copy.21
  66.6 0.1 copy-done
  66.8 0.6 copy.22
Async XLA Ops:
  64.7 1.4 %copy-start.1 = (f32[3,8,192]{2,1,0:T(8,128)S(1)}, f32[3,8,192]{2,1,0:T(8,128)}, u32[]{:S(2)}) copy-start(f32[3,8,192]{2,1,0:T(8,128)} %get-tuple-element.7) | copy-start | bytes 55300
  66.0 0.7 %copy-start = (f32[3,8,192]{2,1,0:T(8,128)S(1)}, f32[3,8,192]{2,1,0:T(8,128)}, u32[]{:S(2)}) copy-start(f32[3,8,192]{2,1,0:T(8,128)} %get-tuple-element.8) | copy-start | bytes 55300

commit v2 on v1

--- a/solution.py
+++ b/solution.py
@@ -14,6 +14,7 @@
 CHUNK = 16
 HALO = 2
 SPLITS = 3
+TERMS = 24
 LOG2E = math.log2(math.e)
 
 step_time = 0.05
@@ -49,7 +50,7 @@
     own_places, own_speeds, feats, w_project, w_filter, w_scale_one, w_invariant, w_magnitude,
     w_later, w_scale_two, w_push,
     place_halo, table_one, table_vec, feat_t, mix, later_t, scale_sq, read_two, s_one, selector,
-    state_x, state_v, state_g, cols, xb, gauss, vecs, mixed,
+    state_x, state_v, state_g, cols, xb, mine, near_w, apart, gauss, vecs, mixed, flats, pushes,
     vg_send, vg_recv, kin_send, kin_recv,
     load_sem, init_send_sem, init_recv_sem, vg_send_sem, vg_recv_sem, kin_send_sem, kin_recv_sem,
 ):
@@ -147,6 +148,7 @@
         for i in range(inner):
             for d in range(3):
                 vecs[p, i, d, near:, :] = jnp.zeros((4 * NA - near, lanes), BF16)
+            near_w[p, i, TERMS * group:, :] = jnp.zeros((LANES - TERMS * group, lanes), BF16)
     feats[ext * NA:, :] = jnp.zeros((wide - ext * NA, channels), BF16)
 
     total = cells * n
@@ -192,7 +194,8 @@
     doubles = [double(signal_tiles, e) for e in range(ext)]
     flat_signals = jnp.concatenate(signal_tiles, axis=1).astype(BF16)
     out = jnp.dot(w_one, flat_signals, preferred_element_type=F32)
-    s_one[...] = out[0:1] + out[1:2]
+    s_one[:, 0:wide] = out[0:1] + out[1:2]
+    s_one[:, wide:] = jnp.zeros((1, LANES), F32)
     for i in range(inner):
         feat_t[i] = double(feat_tiles, i + 1)
         pair = jnp.where(half_lane, doubles[i], doubles[i + 1])
@@ -226,6 +229,19 @@
             for m in range(tiles)
         ]
 
+    def thirds(values):
+        result = []
+        for s in range(SPLITS):
+            piece = values.astype(BF16).astype(F32)
+            values = values - piece
+            result.append(piece)
+        return result
+
+    middle = [0.5, 0.5, 0.5 * cells]
+    eight_row = lax.broadcasted_iota(jnp.int32, (2 * group, lanes), 0)
+    upper = eight_row < group
+    own_lane = eight_row % group == lax.broadcasted_iota(jnp.int32, (2 * group, lanes), 1) // NA
+
     def gather_rows(values, odd):
         result = None
         for r in range(group):
@@ -235,57 +251,93 @@
             result = tile if result is None else jnp.where(member_row == r, tile, result)
         return jnp.broadcast_to(result, (group, LANES))
 
-    def pairs(p, i, place_tiles):
-        e = i + 1
-        mine = [
-            jnp.broadcast_to(jnp.concatenate(spread_row(place_tiles[d], e), axis=1), (CHUNK, lanes))
-            for d in range(3)
-        ]
+    def weigh(p, i, place_tiles):
+        rows = []
+        left_over = None
+        for d in range(3):
+            spread = jnp.concatenate(spread_row(place_tiles[d], i + 1), axis=1)
+            mine[p, i, d] = jnp.broadcast_to(spread, (8, lanes))
+            left_over = 1.0 - spread * spread if left_over is None else left_over - spread * spread
+            rows.append(thirds(2.0 * spread))
+        terms = [three[0] for three in rows for _ in range(SPLITS)]
+        terms += [piece for three in rows for piece in (three[1], three[2], three[1])]
+        terms += [jnp.full((1, lanes), -1.0, F32)] * SPLITS + thirds(left_over)
+        for at in range(0, TERMS, 4):
+            block = jnp.concatenate(
+                [
+                    jnp.where(own_lane, jnp.where(upper, terms[m], terms[m + 1]), 0.0)
+                    for m in (at, at + 2)
+                ],
+                axis=0,
+            )
+            near_w[p, i, at * group:(at + 4) * group, :] = block.astype(BF16)
+
+    def measure(p, i):
+        window = cols[p, i * NA:i * NA + near, :]
+        apart[p, i] = jnp.dot(window, near_w[p, i], preferred_element_type=F32)
+
+    def pairs(p, i):
+        mine_now = [jnp.concatenate([mine[p, i, d]] * (CHUNK // 8), axis=0) for d in range(3)]
         for at in range(0, near, CHUNK):
             row = i * NA + at
-            dx, dy, dz = [xb[p, d, row:row + CHUNK, :] - mine[d] for d in range(3)]
-            squared = dx * dx + dy * dy + dz * dz
-            inside = jnp.maximum(1.0 - squared, 0.0)
+            inside = jnp.maximum(apart[p, i, at:at + CHUNK, :], 0.0)
             envelope = inside * inside
-            for d, step in enumerate((dx, dy, dz)):
+            for d in range(3):
+                step = xb[p, d, row:row + CHUNK, :] - mine_now[d]
                 vecs[p, i, d, at:at + CHUNK, :] = (step * envelope).astype(BF16)
             centered = 0.5 - inside
-            value = jnp.exp2((centered * (centered + 1.0)) * (-98.0 * LOG2E)) * envelope
-            ratio = jnp.exp2(centered * (28.0 * LOG2E))
+            power = (centered * (centered - 1.0 / (basis - 1))) * (-98.0 * LOG2E)
+            start = (jnp.exp2(power) * envelope).astype(BF16)
+            grow = jnp.exp2(centered * (28.0 * LOG2E)).astype(BF16)
+            shrink = jnp.exp2(centered * (-28.0 * LOG2E)).astype(BF16)
+            values = {basis // 2: start}
+            for k in range(basis // 2, basis - 1):
+                values[k + 1] = values[k] * grow
+            for k in range(basis // 2, 0, -1):
+                values[k - 1] = values[k] * shrink
             for k in range(basis):
                 if at < 2 * NA:
                     to = k * LANES + at
                 else:
                     to = basis * LANES + k * NA + at - 2 * NA
-                gauss[p, i, to:to + CHUNK, :] = value.astype(BF16)
-                if k + 1 < basis:
-                    value = value * ratio
-
-    def dense(p, i):
+                gauss[p, i, to:to + CHUNK, :] = values[k]
+
+    def gather_scalar(p, i):
         scalar = jnp.dot(table_one[i], gauss[p, i], preferred_element_type=F32)
         mixed[p, i, 0:channels, :] = scalar.astype(BF16)
+
+    def gather_vector(p, i):
         norm = None
         for d in range(3):
             vec = jnp.dot(table_vec[i], vecs[p, i, d], preferred_element_type=F32)
             norm = vec * vec if norm is None else norm + vec * vec
         norm = norm * jnp.concatenate([scale_sq[...]] * tiles, axis=1)
         mixed[p, i, channels:, :] = norm.astype(BF16)
+
+    def revise(p, i):
         half = jnp.dot(mix[...], mixed[p, i], preferred_element_type=F32)
         hidden = half * jnp.tanh(half) + half + jnp.concatenate([feat_t[i]] * tiles, axis=1)
-        second = jnp.dot(later_t[...], hidden.astype(BF16), preferred_element_type=F32).astype(BF16)
+        return hidden.astype(BF16)
+
+    def project(hidden):
+        return jnp.dot(later_t[...], hidden, preferred_element_type=F32).astype(BF16)
+
+    def read(p, i, second):
         out = jnp.dot(read_two[...], second, preferred_element_type=F32)
-        return out[0:1] + out[1:2]
-
-    def force(p, e, strengths):
-        window = strengths[:, (e - 1) * NA:(e + 3) * NA]
+        flats[p, i] = jnp.broadcast_to(out[0:1] + out[1:2], (8, lanes))
+
+    def force(p, i):
+        even, odd, last = [
+            gather_rows(flats[p, i + j, 0:1, :], odd) for j, odd in ((-1, False), (0, True), (1, False))
+        ]
+        window = jnp.concatenate([jnp.where(half_lane, even, odd), jnp.where(half_lane, last, 0.0)], axis=1)
+        window = window + s_one[:, i * NA:(i + 4) * NA]
         high, low = split_bf16(window)
         stacked = jnp.concatenate([high.astype(F32), low.astype(F32)], axis=0)
         stacked = jnp.concatenate([stacked] * (16 // (2 * group)), axis=0).astype(BF16)
-        result = []
-        for d in range(3):
-            out = jnp.dot(stacked, vecs[p, e - 1, d], preferred_element_type=F32)
-            result.append(gather_rows(out[:group] + out[group:2 * group], e % 2 == 1))
-        return result
+        for d in range(3):
+            out = jnp.dot(stacked, vecs[p, i, d], preferred_element_type=F32)
+            pushes[p, i, d] = gather_rows(out[:group] + out[group:2 * group], i % 2 == 0)
 
     def is_moving(t):
         return jnp.where(t > 0, 1.0, 0.0).astype(F32)
@@ -298,44 +350,62 @@
 
     def advance(t, p):
         moving = is_moving(t)
+        pieces = []
+        square = None
         place_tiles = []
-        stack = []
         for d in range(3):
             half = state_v[p, d] + (0.5 * step_time) * state_g[p, d]
             x = state_x[p, d] + (moving * step_time) * half
             state_v[p, d] = half
             state_x[p, d] = x
+            x = x - middle[d]
             place_tiles.append([x[:, at:at + LANES] for at in range(0, wide, LANES)])
-            rest = x
-            for s in range(SPLITS):
-                piece = rest.astype(BF16).astype(F32)
-                rest = rest - piece
-                stack.append(piece)
-        stack.append(jnp.zeros((LANES - 3 * SPLITS * group, wide), F32))
+            square = x * x if square is None else square + x * x
+            pieces.append(thirds(x))
+        stack = [piece for three in pieces for piece in three]
+        stack += [piece for three in pieces for piece in (three[0], three[0], three[1])]
+        stack += thirds(square)
+        stack += [jnp.ones((SPLITS * group, wide), F32), jnp.zeros((LANES - TERMS * group, wide), F32)]
         tall = jnp.concatenate(stack, axis=0)
         for at in range(0, wide, LANES):
             cols[p, at:at + LANES, :] = tall[:, at:at + LANES].T.astype(BF16)
         for d in range(3):
             xb[p, d] = jnp.dot(cols[p, 0:ext * NA, :], selector[d], preferred_element_type=F32)
-        flats = []
-        for i in range(inner):
-            pairs(p, i, place_tiles)
-            flats.append(dense(p, i))
-        strengths = []
-        for at in range(0, wide // NA, 2):
-            even, odd = [
-                gather_rows(flats[e - 1], e % 2 == 1) if 1 <= e <= inner else jnp.zeros((group, LANES), F32)
-                for e in (at, at + 1)
-            ]
-            strengths.append(jnp.where(half_lane, even, odd))
-        strengths = jnp.concatenate(strengths, axis=1) + s_one[...]
-        pushes = [force(p, e, strengths) for e in range(HALO, HALO + cells)]
+        def stage(i):
+            if i + 1 < inner:
+                weigh(p, i + 1, place_tiles)
+            hidden = revise(p, i - 2) if i >= 2 else None
+            if 1 <= i <= inner:
+                gather_scalar(p, i - 1)
+            if i + 1 < inner:
+                measure(p, i + 1)
+            second = project(hidden) if i >= 2 else None
+            if 1 <= i <= inner:
+                gather_vector(p, i - 1)
+            if i >= 2:
+                read(p, i - 2, second)
+            if i < inner:
+                pairs(p, i)
+
+        weigh(p, 0, place_tiles)
+        measure(p, 0)
+        stage(0)
+        for i in range(1, inner):
+            pl.when(lax.rem((me + i) * (me + i + 1), 2) < 1)(functools.partial(stage, i))
+        stage(inner)
+        for i in range(1, inner - 3):
+            force(p, i)
+        hidden = revise(p, inner - 1)
+        if inner > 3:
+            force(p, inner - 3)
+        read(p, inner - 1, project(hidden))
+        force(p, inner - 2)
         kinetic = jnp.zeros((group, 1), F32)
         for d in range(3):
             joined = []
             for c in range(0, cells, 2):
-                even = pushes[c][d]
-                odd = pushes[c + 1][d] if c + 1 < cells else jnp.zeros((group, LANES), F32)
+                even = pushes[p, c + 1, d]
+                odd = pushes[p, c + 2, d] if c + 1 < cells else jnp.zeros((group, LANES), F32)
                 joined.append(jnp.where(half_lane, even, odd))
             g = jnp.concatenate(joined, axis=1)[:, :own]
             v = state_v[p, d, :, edge:edge + own] + (moving * (0.5 * step_time)) * g
@@ -468,16 +538,21 @@
             pltpu.VMEM((channels, channels), BF16),
             pltpu.VMEM((channels, LANES), F32),
             pltpu.VMEM((16, channels), BF16),
-            pltpu.VMEM((1, wide), F32),
+            pltpu.VMEM((1, wide + LANES), F32),
             pltpu.VMEM((3, LANES, lanes), BF16),
             pltpu.VMEM((parts, 3, group, wide), F32),
             pltpu.VMEM((parts, 3, group, wide), F32),
             pltpu.VMEM((parts, 3, group, wide), F32),
             pltpu.VMEM((parts, wide, LANES), BF16),
             pltpu.VMEM((parts, 3, ext * NA, lanes), F32),
+            pltpu.VMEM((parts, inner, 3, 8, lanes), F32),
+            pltpu.VMEM((parts, inner, LANES, lanes), BF16),
+            pltpu.VMEM((parts, inner, 3 * NA, lanes), F32),
             pltpu.VMEM((parts, inner, depth, lanes), BF16),
             pltpu.VMEM((parts, inner, 3, 4 * NA, lanes), BF16),
             pltpu.VMEM((parts, inner, 2 * channels, lanes), BF16),
+            pltpu.VMEM((parts, inner, 8, lanes), F32),
+            pltpu.VMEM((parts, inner, 3, group, LANES), F32),
             pltpu.VMEM((rounds, parts, 2, 3, group, 2 * edge), F32),
             pltpu.VMEM((rounds, parts, 2, 3, group, 2 * edge), F32),
             pltpu.VMEM((rounds, parts, 1, LANES), F32),

time: 67.7 us -> 65.4 us (0.966)
  Pallas kernels: 64 us -> 61.7 us
    pallas_call x1, Pallas kernels: 64 us -> 61.7 us  [on_device(): pl.pallas_call(functools.partial(kernel, n, replicas, cells, parts), out_...]
where the time goes in v2:
time: 65.4 us; the launch traced here: 65.1 us
  Pallas kernels  61.7 us (94%)
  local copies, waits for them, and re-layouts  2.71 us (4%)
    pallas_call x1, Pallas kernels, on_device(): pl.pallas_call(functools.partial(kernel, n, replicas, cells, parts), out_...  61.7 us
    unnamed x7, local copies, waits for them, and re-layouts  2.71 us

profile of v2, /device:TPU:0, one launch (start us, length us, event | category | flops | bytes accessed | tf_op | source)
XLA Modules:
  0.0 65.1 jit_solution(11662015382502588200)
XLA Ops:
  0.6 61.7 %shard_map.157 = (f32[3,8,192]{2,1,0:T(8,128)}, f32[3,8,192]{2,1,0:T(8,128)}, f32[3,8,192]{2,1,0:T(8,128)}) custom-call(f32[3,8,192]{2,1,0:T(8,128)} %bitcast.11, f32[3,8,192]{2,1,0:T(8,128)} %bitcast.12, f32[8]{0:T(128)} %targets.1, s32[8]{0:T(128)} %slots.1, s32[8]{0:T(128)} %flags.1, bf16[192,128]{1,0:T(8,128)(2,1)} %features.1, ...), custom_call_target="tpu_custom_call" | custom-call | tf_op jit(solution)/shard_map/pallas_call | solution.py:516
  62.4 0.0 copy-start.1
  62.4 1.4 %copy.20 = f32[8,3,192]{2,0,1:T(8,128)} copy(f32[8,3,192]{2,0,1:T(8,128)} %bitcast.10) | data formatting | bytes 36864
  63.7 0.0 copy-done.1
  63.7 0.0 copy-start
  63.7 0.6 copy.21
  64.3 0.1 copy-done
  64.5 0.6 copy.22
Async XLA Ops:
  62.4 1.4 %copy-start.1 = (f32[3,8,192]{2,1,0:T(8,128)S(1)}, f32[3,8,192]{2,1,0:T(8,128)}, u32[]{:S(2)}) copy-start(f32[3,8,192]{2,1,0:T(8,128)} %get-tuple-element.7) | copy-start | bytes 55300
  63.7 0.7 %copy-start = (f32[3,8,192]{2,1,0:T(8,128)S(1)}, f32[3,8,192]{2,1,0:T(8,128)}, u32[]{:S(2)}) copy-start(f32[3,8,192]{2,1,0:T(8,128)} %get-tuple-element.8) | copy-start | bytes 55300

commit v3 on v2

--- a/solution.py
+++ b/solution.py
@@ -49,7 +49,7 @@
     places_out, speeds_out, forces_out,
     own_places, own_speeds, feats, w_project, w_filter, w_scale_one, w_invariant, w_magnitude,
     w_later, w_scale_two, w_push,
-    place_halo, table_one, table_vec, feat_t, mix, later_t, scale_sq, read_two, s_one, selector,
+    place_halo, table_one, table_vec, feat_t, mix, scale_sq, read_two, s_one, selector,
     state_x, state_v, state_g, cols, xb, mine, near_w, apart, gauss, vecs, mixed, flats, pushes,
     vg_send, vg_recv, kin_send, kin_recv,
     load_sem, init_send_sem, init_recv_sem, vg_send_sem, vg_recv_sem, kin_send_sem, kin_recv_sem,
@@ -130,12 +130,15 @@
     filters = (w_filter[...] * jnp.exp(-2.0 * offset * offset)).T
     push_row = w_push[...]
     w_one = weight_rows(w_scale_one[...] * push_row)
-    read_two[...] = weight_rows(w_scale_two[...] * push_row)
+    back = lax.dot_general(
+        weight_rows(w_scale_two[...] * push_row), w_later[...], (((1,), (1,)), ((), ())),
+        preferred_element_type=F32,
+    )
+    read_two[...] = weight_rows(back[0:1] + back[1:2])
     scale_row = jnp.broadcast_to(w_scale_one[...] * w_scale_one[...], (8, channels))
     scale_sq[...] = column(scale_row)
     mix[:, 0:channels] = (0.5 * flip(w_invariant[...])).astype(BF16)
     mix[:, channels:2 * channels] = (0.5 * flip(w_magnitude[...])).astype(BF16)
-    later_t[...] = flip(w_later[...]).astype(BF16)
 
     k_row = lax.broadcasted_iota(jnp.int32, (LANES, lanes), 0)
     k_lane = lax.broadcasted_iota(jnp.int32, (LANES, lanes), 1)
@@ -276,9 +279,9 @@
         window = cols[p, i * NA:i * NA + near, :]
         apart[p, i] = jnp.dot(window, near_w[p, i], preferred_element_type=F32)
 
-    def pairs(p, i):
+    def pairs(p, i, begin, end):
         mine_now = [jnp.concatenate([mine[p, i, d]] * (CHUNK // 8), axis=0) for d in range(3)]
-        for at in range(0, near, CHUNK):
+        for at in range(begin * CHUNK, end * CHUNK, CHUNK):
             row = i * NA + at
             inside = jnp.maximum(apart[p, i, at:at + CHUNK, :], 0.0)
             envelope = inside * inside
@@ -302,15 +305,22 @@
                     to = basis * LANES + k * NA + at - 2 * NA
                 gauss[p, i, to:to + CHUNK, :] = values[k]
 
-    def gather_scalar(p, i):
-        scalar = jnp.dot(table_one[i], gauss[p, i], preferred_element_type=F32)
+    def gather_scalar(p, i, between):
+        depth = table_one.shape[2] // len(between)
+        scalar = None
+        for m, fill in enumerate(between):
+            part = slice(m * depth, (m + 1) * depth)
+            term = jnp.dot(table_one[i, :, part], gauss[p, i, part, :], preferred_element_type=F32)
+            scalar = term if scalar is None else scalar + term
+            fill()
         mixed[p, i, 0:channels, :] = scalar.astype(BF16)
 
-    def gather_vector(p, i):
+    def gather_vector(p, i, between):
         norm = None
         for d in range(3):
             vec = jnp.dot(table_vec[i], vecs[p, i, d], preferred_element_type=F32)
             norm = vec * vec if norm is None else norm + vec * vec
+            between[d]()
         norm = norm * jnp.concatenate([scale_sq[...]] * tiles, axis=1)
         mixed[p, i, channels:, :] = norm.astype(BF16)
 
@@ -319,11 +329,8 @@
         hidden = half * jnp.tanh(half) + half + jnp.concatenate([feat_t[i]] * tiles, axis=1)
         return hidden.astype(BF16)
 
-    def project(hidden):
-        return jnp.dot(later_t[...], hidden, preferred_element_type=F32).astype(BF16)
-
-    def read(p, i, second):
-        out = jnp.dot(read_two[...], second, preferred_element_type=F32)
+    def read(p, i, hidden):
+        out = jnp.dot(read_two[...], hidden, preferred_element_type=F32)
         flats[p, i] = jnp.broadcast_to(out[0:1] + out[1:2], (8, lanes))
 
     def force(p, i):
@@ -372,33 +379,47 @@
         for d in range(3):
             xb[p, d] = jnp.dot(cols[p, 0:ext * NA, :], selector[d], preferred_element_type=F32)
         def stage(i):
+            count = near // CHUNK
+
+            def some(begin, end):
+                if i < inner:
+                    pairs(p, i, count * begin // 12, count * end // 12)
+
+            hidden = revise(p, i - 2) if i >= 2 else None
+            some(0, 1)
+            if 1 <= i <= inner:
+                gather_scalar(p, i - 1, [functools.partial(some, *span) for span in ((1, 2), (2, 3), (3, 4), (4, 5), (5, 6), (6, 6))])
+            else:
+                some(1, 6)
             if i + 1 < inner:
                 weigh(p, i + 1, place_tiles)
-            hidden = revise(p, i - 2) if i >= 2 else None
+                measure(p, i + 1)
+            some(6, 7)
+            if i >= 2:
+                read(p, i - 2, hidden)
+            some(7, 8)
             if 1 <= i <= inner:
-                gather_scalar(p, i - 1)
-            if i + 1 < inner:
-                measure(p, i + 1)
-            second = project(hidden) if i >= 2 else None
-            if 1 <= i <= inner:
-                gather_vector(p, i - 1)
-            if i >= 2:
-                read(p, i - 2, second)
-            if i < inner:
-                pairs(p, i)
+                gather_vector(p, i - 1, [functools.partial(some, *span) for span in ((8, 9), (9, 10), (10, 11))])
+            else:
+                some(8, 11)
+            some(11, 12)
 
         weigh(p, 0, place_tiles)
         measure(p, 0)
         stage(0)
         for i in range(1, inner):
             pl.when(lax.rem((me + i) * (me + i + 1), 2) < 1)(functools.partial(stage, i))
-        stage(inner)
+        empty = [lambda: None] * 3
+        gather_scalar(p, inner - 1, empty[:1])
+        hidden = revise(p, inner - 2)
+        gather_vector(p, inner - 1, empty)
+        read(p, inner - 2, hidden)
         for i in range(1, inner - 3):
             force(p, i)
         hidden = revise(p, inner - 1)
-        if inner > 3:
-            force(p, inner - 3)
-        read(p, inner - 1, project(hidden))
+        for i in range(max(1, inner - 3), inner - 2):
+            force(p, i)
+        read(p, inner - 1, hidden)
         force(p, inner - 2)
         kinetic = jnp.zeros((group, 1), F32)
         for d in range(3):
@@ -535,7 +556,6 @@
             pltpu.VMEM((inner, channels, 4 * NA), BF16),
             pltpu.VMEM((inner, channels, LANES), F32),
             pltpu.VMEM((channels, 2 * channels), BF16),
-            pltpu.VMEM((channels, channels), BF16),
             pltpu.VMEM((channels, LANES), F32),
             pltpu.VMEM((16, channels), BF16),
             pltpu.VMEM((1, wide + LANES), F32),

time: 65.4 us -> 58 us (0.89)
  Pallas kernels: 61.7 us -> 54.4 us
    pallas_call x1, Pallas kernels: 61.7 us -> 54.4 us  [on_device(): pl.pallas_call(functools.partial(kernel, n, replicas, cells, parts), out_...]
where the time goes in v3:
time: 58 us; the launch traced here: 57.8 us
  Pallas kernels  54.4 us (94%)
  local copies, waits for them, and re-layouts  2.71 us (5%)
  between operations  0.65 us (1%)
    pallas_call x1, Pallas kernels, on_device(): pl.pallas_call(functools.partial(kernel, n, replicas, cells, parts), out_...  54.4 us
    unnamed x7, local copies, waits for them, and re-layouts  2.71 us

profile of v3, /device:TPU:0, one launch (start us, length us, event | category | flops | bytes accessed | tf_op | source)
XLA Modules:
  0.0 57.8 jit_solution(5076568239768027635)
XLA Ops:
  0.6 54.4 %shard_map.157 = (f32[3,8,192]{2,1,0:T(8,128)}, f32[3,8,192]{2,1,0:T(8,128)}, f32[3,8,192]{2,1,0:T(8,128)}) custom-call(f32[3,8,192]{2,1,0:T(8,128)} %bitcast.11, f32[3,8,192]{2,1,0:T(8,128)} %bitcast.12, f32[8]{0:T(128)} %targets.1, s32[8]{0:T(128)} %slots.1, s32[8]{0:T(128)} %flags.1, bf16[192,128]{1,0:T(8,128)(2,1)} %features.1, ...), custom_call_target="tpu_custom_call" | custom-call | tf_op jit(solution)/shard_map/pallas_call | solution.py:537
  55.0 0.0 copy-start.1
  55.0 1.4 %copy.20 = f32[8,3,192]{2,0,1:T(8,128)} copy(f32[8,3,192]{2,0,1:T(8,128)} %bitcast.10) | data formatting | bytes 36864
  56.4 0.0 copy-done.1
  56.4 0.0 copy-start
  56.4 0.6 %copy.21 = f32[8,3,192]{2,0,1:T(8,128)} copy(f32[8,3,192]{2,0,1:T(8,128)S(1)} %bitcast.9) | data formatting | bytes 36864
  57.0 0.1 copy-done
  57.1 0.6 %copy.22 = f32[8,3,192]{2,0,1:T(8,128)} copy(f32[8,3,192]{2,0,1:T(8,128)S(1)} %bitcast.8) | data formatting | bytes 36864
Async XLA Ops:
  55.0 1.4 %copy-start.1 = (f32[3,8,192]{2,1,0:T(8,128)S(1)}, f32[3,8,192]{2,1,0:T(8,128)}, u32[]{:S(2)}) copy-start(f32[3,8,192]{2,1,0:T(8,128)} %get-tuple-element.7) | copy-start | bytes 55300
  56.4 0.7 %copy-start = (f32[3,8,192]{2,1,0:T(8,128)S(1)}, f32[3,8,192]{2,1,0:T(8,128)}, u32[]{:S(2)}) copy-start(f32[3,8,192]{2,1,0:T(8,128)} %get-tuple-element.8) | copy-start | bytes 55300

commit v4 on v3

--- a/solution.py
+++ b/solution.py
@@ -407,8 +407,9 @@
         weigh(p, 0, place_tiles)
         measure(p, 0)
         stage(0)
-        for i in range(1, inner):
+        for i in range(1, inner - 1):
             pl.when(lax.rem((me + i) * (me + i + 1), 2) < 1)(functools.partial(stage, i))
+        stage(inner - 1)
         empty = [lambda: None] * 3
         gather_scalar(p, inner - 1, empty[:1])
         hidden = revise(p, inner - 2)
@@ -448,7 +449,11 @@
 
         for copy in vg_copies(t, p):
             copy.start()
-        lax.fori_loop(1, n, spread, 0)
+        if n <= 16:
+            for d in sorted(range(1, n), key=lambda d: min(d, n - d)):
+                spread(d, 0)
+        else:
+            lax.fori_loop(1, n, spread, 0)
 
     def finish(t, p):
         everything = kin_recv.at[t, p, pl.ds(0, n - 1)]

time: 58 us -> 57 us (0.983)
  Pallas kernels: 54.4 us -> 53.4 us
    pallas_call x1, Pallas kernels: 54.4 us -> 53.4 us  [on_device(): pl.pallas_call(functools.partial(kernel, n, replicas, cells, parts), out_...]
where the time goes in v4:
time: 57 us; the launch traced here: 56.8 us
  Pallas kernels  53.4 us (94%)
  local copies, waits for them, and re-layouts  2.71 us (5%)
  between operations  0.65 us (1%)
    pallas_call x1, Pallas kernels, on_device(): pl.pallas_call(functools.partial(kernel, n, replicas, cells, parts), out_...  53.4 us
    unnamed x7, local copies, waits for them, and re-layouts  2.71 us

profile of v4, /device:TPU:0, one launch (start us, length us, event | category | flops | bytes accessed | tf_op | source)
XLA Modules:
  0.0 56.8 jit_solution(1325160628494759053)
XLA Ops:
  0.6 53.4 %shard_map.157 = (f32[3,8,192]{2,1,0:T(8,128)}, f32[3,8,192]{2,1,0:T(8,128)}, f32[3,8,192]{2,1,0:T(8,128)}) custom-call(f32[3,8,192]{2,1,0:T(8,128)} %bitcast.11, f32[3,8,192]{2,1,0:T(8,128)} %bitcast.12, f32[8]{0:T(128)} %targets.1, s32[8]{0:T(128)} %slots.1, s32[8]{0:T(128)} %flags.1, bf16[192,128]{1,0:T(8,128)(2,1)} %features.1, ...), custom_call_target="tpu_custom_call" | custom-call | tf_op jit(solution)/shard_map/pallas_call | solution.py:542
  54.0 0.0 copy-start.1
  54.1 1.4 %copy.20 = f32[8,3,192]{2,0,1:T(8,128)} copy(f32[8,3,192]{2,0,1:T(8,128)} %bitcast.10) | data formatting | bytes 36864
  55.4 0.0 copy-done.1
  55.4 0.0 copy-start
  55.4 0.6 %copy.21 = f32[8,3,192]{2,0,1:T(8,128)} copy(f32[8,3,192]{2,0,1:T(8,128)S(1)} %bitcast.9) | data formatting | bytes 36864
  56.0 0.1 copy-done
  56.2 0.6 %copy.22 = f32[8,3,192]{2,0,1:T(8,128)} copy(f32[8,3,192]{2,0,1:T(8,128)S(1)} %bitcast.8) | data formatting | bytes 36864
Async XLA Ops:
  54.0 1.4 %copy-start.1 = (f32[3,8,192]{2,1,0:T(8,128)S(1)}, f32[3,8,192]{2,1,0:T(8,128)}, u32[]{:S(2)}) copy-start(f32[3,8,192]{2,1,0:T(8,128)} %get-tuple-element.7) | copy-start | bytes 55300
  55.4 0.7 %copy-start = (f32[3,8,192]{2,1,0:T(8,128)S(1)}, f32[3,8,192]{2,1,0:T(8,128)}, u32[]{:S(2)}) copy-start(f32[3,8,192]{2,1,0:T(8,128)} %get-tuple-element.8) | copy-start | bytes 55300

commit v5 on v4

--- a/solution.py
+++ b/solution.py
@@ -49,7 +49,7 @@
     places_out, speeds_out, forces_out,
     own_places, own_speeds, feats, w_project, w_filter, w_scale_one, w_invariant, w_magnitude,
     w_later, w_scale_two, w_push,
-    place_halo, table_one, table_vec, feat_t, mix, scale_sq, read_two, s_one, selector,
+    place_halo, table_one, table_vec, feat_t, mix, read_two, s_one, selector,
     state_x, state_v, state_g, cols, xb, mine, near_w, apart, gauss, vecs, mixed, flats, pushes,
     vg_send, vg_recv, kin_send, kin_recv,
     load_sem, init_send_sem, init_recv_sem, vg_send_sem, vg_recv_sem, kin_send_sem, kin_recv_sem,
@@ -123,9 +123,6 @@
     def flip(values):
         return values.astype(F32).T
 
-    def column(row):
-        return jnp.broadcast_to(row.T[:, 0:1], (channels, LANES))
-
     offset = lax.broadcasted_iota(jnp.int32, (basis, channels), 0).astype(F32) - 0.5 * (basis - 1)
     filters = (w_filter[...] * jnp.exp(-2.0 * offset * offset)).T
     push_row = w_push[...]
@@ -135,10 +132,9 @@
         preferred_element_type=F32,
     )
     read_two[...] = weight_rows(back[0:1] + back[1:2])
-    scale_row = jnp.broadcast_to(w_scale_one[...] * w_scale_one[...], (8, channels))
-    scale_sq[...] = column(scale_row)
     mix[:, 0:channels] = (0.5 * flip(w_invariant[...])).astype(BF16)
-    mix[:, channels:2 * channels] = (0.5 * flip(w_magnitude[...])).astype(BF16)
+    scale_row = w_scale_one[...] * w_scale_one[...]
+    mix[:, channels:2 * channels] = (0.5 * flip(w_magnitude[...]) * scale_row).astype(BF16)
 
     k_row = lax.broadcasted_iota(jnp.int32, (LANES, lanes), 0)
     k_lane = lax.broadcasted_iota(jnp.int32, (LANES, lanes), 1)
@@ -321,7 +317,6 @@
             vec = jnp.dot(table_vec[i], vecs[p, i, d], preferred_element_type=F32)
             norm = vec * vec if norm is None else norm + vec * vec
             between[d]()
-        norm = norm * jnp.concatenate([scale_sq[...]] * tiles, axis=1)
         mixed[p, i, channels:, :] = norm.astype(BF16)
 
     def revise(p, i):
@@ -561,7 +556,6 @@
             pltpu.VMEM((inner, channels, 4 * NA), BF16),
             pltpu.VMEM((inner, channels, LANES), F32),
             pltpu.VMEM((channels, 2 * channels), BF16),
-            pltpu.VMEM((channels, LANES), F32),
             pltpu.VMEM((16, channels), BF16),
             pltpu.VMEM((1, wide + LANES), F32),
             pltpu.VMEM((3, LANES, lanes), BF16),

time: 57 us -> 57 us (level)
  no operation moved by 1% of the time
where the time goes in v5:
time: 57 us; the launch traced here: 56.7 us
  Pallas kernels  53.4 us (94%)
  local copies, waits for them, and re-layouts  2.71 us (5%)
  between operations  0.65 us (1%)
    pallas_call x1, Pallas kernels, on_device(): pl.pallas_call(functools.partial(kernel, n, replicas, cells, parts), out_...  53.4 us
    unnamed x7, local copies, waits for them, and re-layouts  2.71 us

profile of v5, /device:TPU:0, one launch (start us, length us, event | category | flops | bytes accessed | tf_op | source)
XLA Modules:
  0.0 56.7 jit_solution(3791190131848047336)
XLA Ops:
  0.6 53.4 %shard_map.157 = (f32[3,8,192]{2,1,0:T(8,128)}, f32[3,8,192]{2,1,0:T(8,128)}, f32[3,8,192]{2,1,0:T(8,128)}) custom-call(f32[3,8,192]{2,1,0:T(8,128)} %bitcast.11, f32[3,8,192]{2,1,0:T(8,128)} %bitcast.12, f32[8]{0:T(128)} %targets.1, s32[8]{0:T(128)} %slots.1, s32[8]{0:T(128)} %flags.1, bf16[192,128]{1,0:T(8,128)(2,1)} %features.1, ...), custom_call_target="tpu_custom_call" | custom-call | tf_op jit(solution)/shard_map/pallas_call | solution.py:537
  54.0 0.0 copy-start.1
  54.0 1.4 %copy.20 = f32[8,3,192]{2,0,1:T(8,128)} copy(f32[8,3,192]{2,0,1:T(8,128)} %bitcast.10) | data formatting | bytes 36864
  55.4 0.0 copy-done.1
  55.4 0.0 copy-start
  55.4 0.6 %copy.21 = f32[8,3,192]{2,0,1:T(8,128)} copy(f32[8,3,192]{2,0,1:T(8,128)S(1)} %bitcast.9) | data formatting | bytes 36864
  56.0 0.1 copy-done
  56.1 0.6 %copy.22 = f32[8,3,192]{2,0,1:T(8,128)} copy(f32[8,3,192]{2,0,1:T(8,128)S(1)} %bitcast.8) | data formatting | bytes 36864
Async XLA Ops:
  54.0 1.4 %copy-start.1 = (f32[3,8,192]{2,1,0:T(8,128)S(1)}, f32[3,8,192]{2,1,0:T(8,128)}, u32[]{:S(2)}) copy-start(f32[3,8,192]{2,1,0:T(8,128)} %get-tuple-element.7) | copy-start | bytes 55300
  55.4 0.7 %copy-start = (f32[3,8,192]{2,1,0:T(8,128)S(1)}, f32[3,8,192]{2,1,0:T(8,128)}, u32[]{:S(2)}) copy-start(f32[3,8,192]{2,1,0:T(8,128)} %get-tuple-element.8) | copy-start | bytes 55300
